TPU v7x, 256 devices: a whole 4x4x8 slice. The times are simulated.
256 devices in a mesh: dp: 32 (over y, z), vocab: 8 (over x, core).
Axes of the slice: x: 4, y: 4, z: 8, core: 2. Of those that a mesh axis runs over, the one named last changes fastest.
Arguments:
- hidden: bfloat16 [24576, 2048], P('dp', 'vocab')
- gain: bfloat16 [2048], replicated, may hold values from 0.5 to 1.5
- head: bfloat16 [2048, 32000], P('dp', 'vocab')
- target_ids: int32 [24576], P('dp'), may hold values from 0 to 31999
- seq_lens: int32 [64], replicated, may hold values from 64 to 704, as said below
- seq_owner: int32 [64], replicated, may hold values from 0 to 31, as said below
Outputs:
- logprob: float32 [24576], P('dp')
- entropy: float32 [24576], P('dp')
Inputs may be any that keep to these rules, and one draw needn't show every extreme that they name: `seq_lens`: the lengths of the sequences owned by one dp index sum to at most 768; in every draw the sequences of some dp index sum to exactly 768. `seq_owner`: every dp index owns exactly 2 sequences.
All inputs are finite; a program needn't handle non-finite values.
Results may differ from a plain program's by a relative error of at most 0.0075.
Values may be sent and summed in bfloat16 or wider, within the bound.
A program may use at most 64 MiB of HBM per device.

v0:
```python
import jax
import jax.numpy as jnp
from jax import lax
from jax.sharding import PartitionSpec as P

EPS = 1e-05


def chunk_bounds(breadth, parts):
    step = -(-breadth // parts)
    step = -(-step // 128) * 128
    bounds = []
    start = 0
    while start < breadth:
        stop = min(start + step, breadth)
        bounds.append((start, stop))
        start = stop
    return bounds


def chunk_stats(normed, columns, local_id, start):
    logits = jnp.dot(normed, columns, preferred_element_type=jnp.float32)
    top = jnp.max(logits, axis=1)
    expo = jnp.exp(logits - top[:, None])
    total = jnp.sum(expo, axis=1)
    weighted = jnp.sum(expo * logits, axis=1)
    ids = start + lax.broadcasted_iota(jnp.int32, logits.shape, 1)
    picked = jnp.sum(jnp.where(ids == local_id[:, None], logits, 0.0), axis=1)
    return (top, total, weighted, picked)


def local(hidden, gain, head, target_ids, seq_lens, seq_owner):
    groups = lax.axis_size("dp")
    position = lax.axis_index("dp")
    slice_index = lax.axis_index("vocab")
    slots = hidden.shape[0]
    breadth = head.shape[1]
    owners = jnp.arange(groups, dtype=jnp.int32)
    loads = jnp.sum(jnp.where(seq_owner[:, None] == owners[None, :], seq_lens[:, None], 0), axis=0)
    own_live = jnp.arange(slots, dtype=jnp.int32) < loads[position]
    features = lax.all_gather(hidden, "vocab", axis=1, tiled=True)
    wide = features.astype(jnp.float32)
    normed = (
        wide
        * lax.rsqrt(jnp.mean(wide * wide, axis=1, keepdims=True) + EPS)
        * gain.astype(jnp.float32)
    ).astype(jnp.bfloat16)
    local_id = target_ids - slice_index * breadth
    parts = []
    for start, stop in chunk_bounds(breadth, 4):
        columns = lax.all_gather(head[:, start:stop], "dp", axis=0, tiled=True)
        parts.append(chunk_stats(normed, columns, local_id, start))
    tops = jnp.stack([p[0] for p in parts])
    top_local = jnp.max(tops, axis=0)
    scale = jnp.exp(tops - top_local[None, :])
    total_local = jnp.sum(jnp.stack([p[1] for p in parts]) * scale, axis=0)
    weighted_local = jnp.sum(jnp.stack([p[2] for p in parts]) * scale, axis=0)
    picked_local = jnp.sum(jnp.stack([p[3] for p in parts]), axis=0)
    top = lax.pmax(top_local, "vocab")
    factor = jnp.exp(top_local - top)
    total, weighted, picked = lax.psum(
        (total_local * factor, weighted_local * factor, picked_local), "vocab"
    )
    lse = top + jnp.log(total)
    logprob = picked - lse
    entropy = lse - weighted / total
    return (jnp.where(own_live, logprob, 0.0), jnp.where(own_live, entropy, 0.0))


def solution(mesh):
    return jax.shard_map(
        local,
        mesh=mesh,
        in_specs=(P("dp", "vocab"), P(), P("dp", "vocab"), P("dp"), P(), P()),
        out_specs=(P("dp"), P("dp")),
        check_vma=False,
    )
```

profile of v0, /device:TPU:32, one launch (start us, length us, event | category | flops | bytes accessed | tf_op | source)
XLA Modules:
  0.0 432.0 jit_solution(7421292452426967437)
XLA Ops:
  7.2 0.0 all-gather.6.cloned.1.call-start
  7.2 0.7 all-gather.6.cloned.1.call-update
  7.9 0.0 all-gather.14.cloned.1.call-start
  7.9 1.6 slice.15
  9.5 0.0 all-gather.14.cloned.1.call-update
  9.5 0.0 all-gather.8.cloned.1.call-start
  9.6 1.8 fusion.20
  11.4 0.0 all-gather.8.cloned.1.call-update
  11.4 0.0 all-gather.10.cloned.1.call-start
  11.5 0.5 all-gather.10.cloned.1.call-update
  12.0 0.0 all-gather.12.cloned.1.call-start
  12.0 0.5 all-gather.12.cloned.1.call-update
  12.6 0.7 convert_element_type.10
  13.3 0.8 select_reduce_fusion.4
  14.1 0.7 dynamic_slice.3
  14.7 0.7 broadcast_subtract_fusion
  15.4 31.2 %all-gather.6.cloned.1.call-done = bf16[768,2048]{1,0:T(8,128)(2,1)} async-done(((bf16[768,256]{1,0:T(8,128)(2,1)}), bf16[768,2048]{1,0:T(8,128)(2,1)}) %all-gather.6.cloned.1.call-update) | async-done | bytes 3145744 | tf_op jit(solution)/shard_map/all_gather | solution.py:41
  46.6 0.0 copy-start.1
  46.6 2.7 fusion
  49.4 82.9 %all-gather.14.cloned.1.call-done = bf16[2048,928]{1,0:T(8,128)(2,1)} async-done(((bf16[64,928]{1,0:T(8,128)(2,1)}), bf16[2048,928]{1,0:T(8,128)(2,1)}) %all-gather.14.cloned.1.call-update) | async-done | bytes 3801104 | tf_op jit(solution)/shard_map/all_gather | solution.py:51
  132.3 0.0 copy-done.1
  132.3 5.9 %fusion.21 = (f32[768]{0:T(1024)S(1)}, f32[768,928]{0,1:T(8,128)S(1)}) fusion(bf16[2048,928]{1,0:T(8,128)(2,1)} %all-gather.14.cloned.1.call-done, bf16[768,2048]{1,0:T(8,128)(2,1)S(1)} %copy-done.1, f32[2048]{0:T(1024)S(1)} %convert_element_type.10, f32[768]{0:T(1024)S(1)} %add_rsqrt_fusion), kind=kOutput, calls=%fused_computation.49 | convolution fusion | flops 2926238976 | bytes 9811968 | tf_op jit(solution)/shard_map/dot_general | solution.py:22
  138.2 0.9 multiply_reduce_fusion.3
  139.0 74.9 %all-gather.8.cloned.1.call-done = bf16[2048,1024]{1,0:T(8,128)(2,1)} async-done(((bf16[64,1024]{1,0:T(8,128)(2,1)}), bf16[2048,1024]{1,0:T(8,128)(2,1)}) %all-gather.8.cloned.1.call-update) | async-done | bytes 4194320 | tf_op jit(solution)/shard_map/all_gather | solution.py:51
  214.0 6.4 %fusion.24 = (f32[768]{0:T(1024)S(1)}, f32[768,1024]{1,0:T(8,128)S(1)}) fusion(bf16[2048,1024]{1,0:T(8,128)(2,1)} %all-gather.8.cloned.1.call-done, bf16[768,2048]{1,0:T(8,128)(2,1)} %all-gather.6.cloned.1.call-done, f32[2048]{0:T(1024)S(1)} %convert_element_type.10, f32[768]{0:T(1024)S(1)} %add_rsqrt_fusion), kind=kOutput, calls=%fused_computation.52 | convolution fusion | flops 3228302592 | bytes 10500096 | tf_op jit(solution)/shard_map/dot_general | solution.py:22
  220.4 75.1 %all-gather.10.cloned.1.call-done = bf16[2048,1024]{1,0:T(8,128)(2,1)} async-done(((bf16[64,1024]{1,0:T(8,128)(2,1)}), bf16[2048,1024]{1,0:T(8,128)(2,1)}) %all-gather.10.cloned.1.call-update) | async-done | bytes 4194320 | tf_op jit(solution)/shard_map/all_gather | solution.py:51
  295.5 8.4 %fusion.22 = (f32[768]{0:T(1024)S(1)}, f32[768,1024]{1,0:T(8,128)}) fusion(bf16[2048,1024]{1,0:T(8,128)(2,1)} %all-gather.10.cloned.1.call-done, bf16[768,2048]{1,0:T(8,128)(2,1)} %all-gather.6.cloned.1.call-done, f32[2048]{0:T(1024)S(1)} %convert_element_type.10, f32[768]{0:T(1024)S(1)} %add_rsqrt_fusion), kind=kOutput, calls=%fused_computation.50 | convolution fusion | flops 3228302592 | bytes 10500096 | tf_op jit(solution)/shard_map/dot_general | solution.py:22
  303.8 73.2 %all-gather.12.cloned.1.call-done = bf16[2048,1024]{1,0:T(8,128)(2,1)} async-done(((bf16[64,1024]{1,0:T(8,128)(2,1)}), bf16[2048,1024]{1,0:T(8,128)(2,1)}) %all-gather.12.cloned.1.call-update) | async-done | bytes 4194320 | tf_op jit(solution)/shard_map/all_gather | solution.py:51
  377.0 0.0 copy-start
  377.0 6.6 %fusion.23 = (f32[768]{0:T(1024)S(1)}, f32[768,1024]{1,0:T(8,128)S(1)}) fusion(bf16[2048,1024]{1,0:T(8,128)(2,1)} %all-gather.12.cloned.1.call-done, bf16[768,2048]{1,0:T(8,128)(2,1)} %all-gather.6.cloned.1.call-done, f32[2048]{0:T(1024)S(1)} %convert_element_type.10, f32[768]{0:T(1024)S(1)} %add_rsqrt_fusion), kind=kOutput, calls=%fused_computation.51 | convolution fusion | flops 3228302592 | bytes 10500096 | tf_op jit(solution)/shard_map/dot_general | solution.py:22
  383.6 0.0 copy-done
  383.6 4.4 %multiply_reduce_fusion.1 = (f32[768]{0:T(1024)S(1)}, f32[768]{0:T(1024)S(1)}, f32[768]{0:T(1024)S(1)}, f32[768]{0:T(1024)S(1)}, f32[768]{0:T(1024)S(1)}, /*inde...) fusion(f32[768,1024]{1,0:T(8,128)S(1)} %copy-done, f32[768]{0:T(1024)S(1)} %get-tuple-element.34, ...), kind=kLoop, calls=%fused_computation.6 | loop fusion | flops 16508160 | bytes 9485312 | tf_op jit(solution)/shard_map/reduce_sum | solution.py:26
  388.1 12.4 %pmax.7 = f32[768]{0:T(1024)S(1)} all-reduce(f32[768]{0:T(1024)S(1)} %maximum_maximum_fusion), channel_id=1, replica_groups=mesh['dp'=32,'vocab'=8] {'vocab'}, use_global_device_ids=true, to_apply=%region_11.12 | all-reduce | flops 768 | bytes 6144 | tf_op jit(solution)/shard_map/pmax | solution.py:59
  400.5 0.1 fusion.9
  400.6 23.6 %all-reduce = (f32[768]{0:T(1024)S(1)}, f32[768]{0:T(1024)S(1)}, f32[768]{0:T(1024)S(1)}) all-reduce(f32[768]{0:T(1024)S(1)} %add_add_fusion, f32[768]{0:T(1024)S(1)} %get-tuple-element.25, f32[768]{0:T(1024)S(1)} %get-tuple-element.24), channel_id=1, replica_groups=mesh['dp'=32,'vocab'=8] {'vocab'}, use_global_device_ids=true, to_apply=%region_6.7 | all-reduce | flops 2304 | bytes 18432 | tf_op jit(solution)/shard_map/psum | solution.py:61
  424.2 1.3 subtract_select_fusion
  (18 shorter events, 0.1 us)
Async XLA Ops:
  7.2 39.5 %all-gather.6.cloned.1.call-start = ((), (), s32[]{:S(2)}) async-start(), calls=%async_computation | async-start | bytes 3538944 | tf_op jit(solution)/shard_map/all_gather | solution.py:41
  7.9 124.4 %all-gather.14.cloned.1.call-start = ((), (), s32[]{:S(2)}) async-start(), calls=%async_computation.4 | async-start | bytes 4325376 | tf_op jit(solution)/shard_map/all_gather | solution.py:51
  9.5 204.4 %all-gather.8.cloned.1.call-start = ((), (), s32[]{:S(2)}) async-start(), calls=%async_computation.1 | async-start | bytes 4325376 | tf_op jit(solution)/shard_map/all_gather | solution.py:51
  11.4 284.1 %all-gather.10.cloned.1.call-start = ((), (), s32[]{:S(2)}) async-start(), calls=%async_computation.2 | async-start | bytes 4325376 | tf_op jit(solution)/shard_map/all_gather | solution.py:51
  12.0 365.0 %all-gather.12.cloned.1.call-start = ((), (), s32[]{:S(2)}) async-start(), calls=%async_computation.3 | async-start | bytes 4325376 | tf_op jit(solution)/shard_map/all_gather | solution.py:51
  46.6 85.6 %copy-start.1 = (bf16[768,2048]{1,0:T(8,128)(2,1)S(1)}, bf16[768,2048]{1,0:T(8,128)(2,1)}, u32[]{:S(2)}) copy-start(bf16[768,2048]{1,0:T(8,128)(2,1)} %all-gather.6.cloned.1.call-done) | copy-start | bytes 9437188
  377.0 6.6 %copy-start = (f32[768,1024]{1,0:T(8,128)S(1)}, f32[768,1024]{1,0:T(8,128)}, u32[]{:S(2)}) copy-start(f32[768,1024]{1,0:T(8,128)} %get-tuple-element.35) | copy-start | bytes 9437188
Sparse Core Ops, SparseCore 0:
  9.8 36.7 all-gather.5
  49.2 83.0 all-gather.13
  134.9 79.0 all-gather.7
  216.4 79.0 all-gather.9
  297.9 79.0 all-gather.11
where the time goes:
time: 432 us
  waiting for transfers between devices  339 us (78%)
  blocking collectives  36 us (8%)
  matrix products  27.2 us (6%)
  between operations  13.9 us (3%)
  other arithmetic  11.6 us (3%)
    all_gather x4, waiting for transfers between devices, local(): columns = lax.all_gather(head[:, start:stop], 'dp', axis=0, tiled=True)  306 us
    all_gather x1, waiting for transfers between devices, local(): features = lax.all_gather(hidden, 'vocab', axis=1, tiled=True)  31.2 us
    dot_general x4, matrix products, chunk_stats(): logits = jnp.dot(normed, columns, preferred_element_type=jnp.float32)  27.2 us
    psum x1, blocking collectives, local(): lax.psum((total_local * factor, weighted_local * factor, picked_local), '...  23.6 us
    pmax x1, blocking collectives, local(): top = lax.pmax(top_local, 'vocab')  12.4 us
  transfers between devices with their start and end apart: 5, of which 5 were waited for; matrix products, arithmetic and copies ran while one was open for 7% of the time, Pallas kernels for 0%

commit v1 on v0

--- a/solution.py
+++ b/solution.py
@@ -48,7 +48,10 @@
     local_id = target_ids - slice_index * breadth
     parts = []
     for start, stop in chunk_bounds(breadth, 4):
-        columns = lax.all_gather(head[:, start:stop], "dp", axis=0, tiled=True)
+        columns = jnp.concatenate(
+            lax.all_to_all(jnp.stack([head[:, start:stop]] * lax.axis_size("dp")), "dp", 0, 0),
+            axis=0,
+        )
         parts.append(chunk_stats(normed, columns, local_id, start))
     tops = jnp.stack([p[0] for p in parts])
     top_local = jnp.max(tops, axis=0)

time: 432 us -> 485 us (1.12)
  blocking collectives: 36 us -> 141 us
  waiting for transfers between devices: 339 us -> 264 us
  starting transfers between devices: 0.2 us -> 23.5 us
  local copies, waits for them, and re-layouts: 4.11 us -> 9.7 us
    all_gather x4 -> x0, waiting for transfers between devices: 306 us -> none  [local(): columns = lax.all_gather(head[:, start:stop], 'dp', axis=0, tiled=True)]
    all_to_all x0 -> x3, waiting for transfers between devices: none -> 263 us  [local(): lax.all_to_all(jnp.stack([head[:, start:stop]] * lax.axis_size('dp')), 'd...]
    all_to_all x0 -> x1, blocking collectives: none -> 102 us  [local(): lax.all_to_all(jnp.stack([head[:, start:stop]] * lax.axis_size('dp')), 'd...]
    all_gather x1, waiting for transfers between devices: 31.2 us -> 0.02 us  [local(): features = lax.all_gather(hidden, 'vocab', axis=1, tiled=True)]
    all_to_all x0 -> x3, starting transfers between devices: none -> 23.5 us  [local(): lax.all_to_all(jnp.stack([head[:, start:stop]] * lax.axis_size('dp')), 'd...]
    another operation x0 -> x4, local copies, waits for them, and re-layouts: none -> 7.98 us  [local(): jnp.stack([head[:, start:stop]] * lax.axis_size('dp'))]
  transfers between devices with their start and end apart: 5 -> 4, of which waited for: 5 -> 3; matrix products, arithmetic and copies ran while one was open for 7% -> 5% of each run, Pallas kernels for 0% -> 0%
where the time goes in v1:
time: 485 us; the launch traced here: 484 us
  waiting for transfers between devices  264 us (54%)
  blocking collectives  141 us (29%)
  starting transfers between devices  23.5 us (5%)
  matrix products  23.2 us (5%)
  between operations  14.3 us (3%)
  local copies, waits for them, and re-layouts  9.7 us (2%)
  other arithmetic  9.24 us (2%)
    all_to_all x3, waiting for transfers between devices, local(): lax.all_to_all(jnp.stack([head[:, start:stop]] * lax.axis_size('dp')), 'd...  263 us
    all_to_all x1, blocking collectives, local(): lax.all_to_all(jnp.stack([head[:, start:stop]] * lax.axis_size('dp')), 'd...  102 us
    psum x1, blocking collectives, local(): lax.psum((total_local * factor, weighted_local * factor, picked_local), '...  23.6 us
    all_to_all x3, starting transfers between devices, local(): lax.all_to_all(jnp.stack([head[:, start:stop]] * lax.axis_size('dp')), 'd...  23.5 us
    dot_general x4, matrix products, chunk_stats(): logits = jnp.dot(normed, columns, preferred_element_type=jnp.float32)  23.2 us
    pmax x1, blocking collectives, local(): top = lax.pmax(top_local, 'vocab')  14.7 us
  transfers between devices with their start and end apart: 4, of which 3 were waited for; matrix products, arithmetic and copies ran while one was open for 5% of the time, Pallas kernels for 0%

profile of v1, /device:TPU:32, one launch (start us, length us, event | category | flops | bytes accessed | tf_op | source)
XLA Modules:
  0.0 484.1 jit_solution(6710098460293923704)
XLA Ops:
  7.2 0.9 slice.15
  8.1 2.5 stack.41
  10.6 0.0 copy-start.3
  10.6 11.5 %all-to-all-start.3 = ((bf16[32,64,928]{2,1,0:T(8,128)(2,1)}), bf16[32,64,928]{2,1,0:T(8,128)(2,1)}, u32[]{:S(2)}, u32[]{:S(2)}) async-start(bf16[32,64,928]{2,1,0:T(8,128)(2,1)} %stack.41), calls=%async_computation.3 | async-start | bytes 8388608 | tf_op jit(solution)/shard_map/all_to_all | solution.py:52
  22.1 0.0 copy-done.3
  22.2 95.5 %all-to-all-done.3 = bf16[32,64,928]{2,1,0:T(8,128)(2,1)} async-done(((bf16[32,64,928]{2,1,0:T(8,128)(2,1)}), bf16[32,64,928]{2,1,0:T(8,128)(2,1)}, u32[]{:S(2)}, u32[]{:S(2)}) %all-to-all-start.3) | async-done | bytes 3801120 | tf_op jit(solution)/shard_map/all_to_all | solution.py:52
  117.7 0.5 stack.39
  118.2 102.4 %all_to_all.20 = bf16[32,64,1024]{2,1,0:T(8,128)(2,1)} all-to-all(bf16[32,64,1024]{2,1,0:T(8,128)(2,1)S(1)} %stack.39), channel_id=1, replica_groups=mesh['dp'=32,'vocab'=8] {'dp'}, dimensions={0} | all-to-all | bytes 8388608 | tf_op jit(solution)/shard_map/all_to_all | solution.py:52
  220.6 2.5 stack.38
  223.1 5.2 %all-to-all-start = ((bf16[32,64,1024]{2,1,0:T(8,128)(2,1)}), bf16[32,64,1024]{2,1,0:T(8,128)(2,1)}, u32[]{:S(2)}, u32[]{:S(2)}) async-start(bf16[32,64,1024]{2,1,0:T(8,128)(2,1)} %stack.38), calls=%async_computation | async-start | bytes 8388608 | tf_op jit(solution)/shard_map/all_to_all | solution.py:52
  228.3 0.0 all-gather.2.cloned.1.call-start
  228.4 0.7 all-gather.2.cloned.1.call-update
  229.1 94.3 %all-to-all-done = bf16[32,64,1024]{2,1,0:T(8,128)(2,1)} async-done(((bf16[32,64,1024]{2,1,0:T(8,128)(2,1)}), bf16[32,64,1024]{2,1,0:T(8,128)(2,1)}, u32[]{:S(2)}, u32[]{:S(2)}) %all-to-all-start) | async-done | bytes 4194336 | tf_op jit(solution)/shard_map/all_to_all | solution.py:52
  323.4 2.5 stack.40
  325.8 0.0 copy-start.4
  325.8 0.0 copy-start.6
  325.8 0.0 copy-start.7
  325.8 0.0 copy-start.5
  325.8 6.7 %all-to-all-start.2 = ((bf16[32,64,1024]{2,1,0:T(8,128)(2,1)}), bf16[32,64,1024]{2,1,0:T(8,128)(2,1)}, u32[]{:S(2)}, u32[]{:S(2)}) async-start(bf16[32,64,1024]{2,1,0:T(8,128)(2,1)} %stack.40), calls=%async_computation.2 | async-start | bytes 8388608 | tf_op jit(solution)/shard_map/all_to_all | solution.py:52
  332.5 0.0 copy-done.4
  332.5 0.0 copy-done.6
  332.5 0.0 copy-done.7
  332.6 0.1 select_reduce_fusion.4
  332.7 0.6 dynamic_slice.3
  333.3 0.0 copy-done.5
  333.3 0.0 all-gather.2.cloned.1.call-done
  333.3 0.0 copy-start.2
  333.3 2.7 fusion
  336.1 0.1 copy-done.2
  336.1 5.8 %fusion.21 = (f32[768]{0:T(1024)S(1)}, f32[768,928]{0,1:T(8,128)S(1)}) fusion(bf16[2048,928]{1,0:T(8,128)(2,1)} %bitcast.4, bf16[768,2048]{1,0:T(8,128)(2,1)S(1)} %copy-done.2, f32[2048]{0:T(1024)S(1)} %convert_element_type.10, f32[768]{0:T(1024)S(1)} %add_rsqrt_fusion), kind=kOutput, calls=%fused_computation.49 | convolution fusion | flops 2926238976 | bytes 9811968 | tf_op jit(solution)/shard_map/dot_general | solution.py:22
  342.0 0.9 multiply_reduce_fusion.3
  342.9 0.0 copy-start
  342.9 5.6 %fusion.24 = (f32[768]{0:T(1024)S(1)}, f32[768,1024]{1,0:T(8,128)S(1)}) fusion(bf16[2048,1024]{1,0:T(8,128)(2,1)} %bitcast.1, bf16[768,2048]{1,0:T(8,128)(2,1)S(1)} %copy-done.2, f32[2048]{0:T(1024)S(1)} %convert_element_type.10, f32[768]{0:T(1024)S(1)} %add_rsqrt_fusion), kind=kOutput, calls=%fused_computation.52 | convolution fusion | flops 3228302592 | bytes 10500096 | tf_op jit(solution)/shard_map/dot_general | solution.py:22
  348.5 0.0 copy-done
  348.6 5.2 %fusion.22 = (f32[768]{0:T(1024)S(1)}, f32[768,1024]{1,0:T(8,128)}) fusion(bf16[2048,1024]{1,0:T(8,128)(2,1)S(1)} %bitcast.9, bf16[768,2048]{1,0:T(8,128)(2,1)S(1)} %copy-done.2, f32[2048]{0:T(1024)S(1)} %convert_element_type.10, f32[768]{0:T(1024)S(1)} %add_rsqrt_fusion), kind=kOutput, calls=%fused_computation.50 | convolution fusion | flops 3228302592 | bytes 10500096 | tf_op jit(solution)/shard_map/dot_general | solution.py:22
  353.7 73.1 %all-to-all-done.2 = bf16[32,64,1024]{2,1,0:T(8,128)(2,1)} async-done(((bf16[32,64,1024]{2,1,0:T(8,128)(2,1)}), bf16[32,64,1024]{2,1,0:T(8,128)(2,1)}, u32[]{:S(2)}, u32[]{:S(2)}) %all-to-all-start.2) | async-done | bytes 4194336 | tf_op jit(solution)/shard_map/all_to_all | solution.py:52
  426.8 0.0 copy-start.1
  426.8 6.5 %fusion.23 = (f32[768]{0:T(1024)S(1)}, f32[768,1024]{1,0:T(8,128)S(1)}) fusion(bf16[2048,1024]{1,0:T(8,128)(2,1)} %bitcast.3, bf16[768,2048]{1,0:T(8,128)(2,1)} %all-gather.2.cloned.1.call-done, f32[2048]{0:T(1024)S(1)} %convert_element_type.10, f32[768]{0:T(1024)S(1)} %add_rsqrt_fusion), kind=kOutput, calls=%fused_computation.51 | convolution fusion | flops 3228302592 | bytes 10500096 | tf_op jit(solution)/shard_map/dot_general | solution.py:22
  433.4 0.0 copy-done.1
  433.4 4.3 multiply_reduce_fusion.1
  437.7 14.7 %pmax.7 = f32[768]{0:T(1024)S(1)} all-reduce(f32[768]{0:T(1024)S(1)} %maximum_maximum_fusion), channel_id=1, replica_groups=mesh['dp'=32,'vocab'=8] {'vocab'}, use_global_device_ids=true, to_apply=%region_11.12 | all-reduce | flops 768 | bytes 6144 | tf_op jit(solution)/shard_map/pmax | solution.py:62
  452.4 0.1 fusion.9
  452.5 23.6 %all-reduce = (f32[768]{0:T(1024)S(1)}, f32[768]{0:T(1024)S(1)}, f32[768]{0:T(1024)S(1)}) all-reduce(f32[768]{0:T(1024)S(1)} %add_add_fusion, f32[768]{0:T(1024)S(1)} %get-tuple-element.25, f32[768]{0:T(1024)S(1)} %get-tuple-element.24), channel_id=1, replica_groups=mesh['dp'=32,'vocab'=8] {'vocab'}, use_global_device_ids=true, to_apply=%region_6.7 | all-reduce | flops 2304 | bytes 18432 | tf_op jit(solution)/shard_map/psum | solution.py:64
  476.1 1.2 subtract_select_fusion
  (21 shorter events, 0.1 us)
Async XLA Ops:
  10.6 11.6 %copy-start.3 = (bf16[64,4000]{1,0:T(8,128)(2,1)S(1)}, bf16[64,4000]{1,0:T(8,128)(2,1)}, u32[]{:S(2)}) copy-start(bf16[64,4000]{1,0:T(8,128)(2,1)} %param.8) | copy-start | bytes 1536004
  10.6 107.1 %all-to-all-start.3 = ((bf16[32,64,928]{2,1,0:T(8,128)(2,1)}), bf16[32,64,928]{2,1,0:T(8,128)(2,1)}, u32[]{:S(2)}, u32[]{:S(2)}) async-start(bf16[32,64,928]{2,1,0:T(8,128)(2,1)} %stack.41), calls=%async_computation.3 | async-start | bytes 8388608 | tf_op jit(solution)/shard_map/all_to_all | solution.py:52
  223.1 100.3 %all-to-all-start = ((bf16[32,64,1024]{2,1,0:T(8,128)(2,1)}), bf16[32,64,1024]{2,1,0:T(8,128)(2,1)}, u32[]{:S(2)}, u32[]{:S(2)}) async-start(bf16[32,64,1024]{2,1,0:T(8,128)(2,1)} %stack.38), calls=%async_computation | async-start | bytes 8388608 | tf_op jit(solution)/shard_map/all_to_all | solution.py:52
  228.3 105.0 %all-gather.2.cloned.1.call-start = ((), (), s32[]{:S(2)}) async-start(), calls=%async_computation.4 | async-start | bytes 3538944 | tf_op jit(solution)/shard_map/all_gather | solution.py:41
  325.8 6.7 %copy-start.4 = (bf16[2048]{0:T(1024)(128)(2,1)S(1)}, bf16[2048]{0:T(1024)(128)(2,1)}, u32[]{:S(2)}) copy-start(bf16[2048]{0:T(1024)(128)(2,1)} %param.7) | copy-start | bytes 12292
  325.8 6.7 %copy-start.6 = (s32[64]{0:T(128)S(1)}, s32[64]{0:T(128)}, u32[]{:S(2)}) copy-start(s32[64]{0:T(128)} %param.10) | copy-start | bytes 772
  325.8 6.7 %copy-start.7 = (s32[64]{0:T(128)S(1)}, s32[64]{0:T(128)}, u32[]{:S(2)}) copy-start(s32[64]{0:T(128)} %param.11) | copy-start | bytes 772
  325.8 7.4 %copy-start.5 = (s32[768]{0:T(1024)S(1)}, s32[768]{0:T(1024)}, u32[]{:S(2)}) copy-start(s32[768]{0:T(1024)} %param.9) | copy-start | bytes 9220
  325.8 100.9 %all-to-all-start.2 = ((bf16[32,64,1024]{2,1,0:T(8,128)(2,1)}), bf16[32,64,1024]{2,1,0:T(8,128)(2,1)}, u32[]{:S(2)}, u32[]{:S(2)}) async-start(bf16[32,64,1024]{2,1,0:T(8,128)(2,1)} %stack.40), calls=%async_computation.2 | async-start | bytes 8388608 | tf_op jit(solution)/shard_map/all_to_all | solution.py:52
  333.3 2.8 copy-start.2
  342.9 5.7 %copy-start = (bf16[32,64,1024]{2,1,0:T(8,128)(2,1)S(1)}, bf16[32,64,1024]{2,1,0:T(8,128)(2,1)}, u32[]{:S(2)}) copy-start(bf16[32,64,1024]{2,1,0:T(8,128)(2,1)} %all_to_all.20) | copy-start | bytes 12582916
  426.8 6.6 %copy-start.1 = (f32[768,1024]{1,0:T(8,128)S(1)}, f32[768,1024]{1,0:T(8,128)}, u32[]{:S(2)}) copy-start(f32[768,1024]{1,0:T(8,128)} %get-tuple-element.35) | copy-start | bytes 9437188
Sparse Core Ops, SparseCore 0:
  231.0 35.1 all-gather.1
